TPU v7x, 32 devices: a whole 2x2x4 slice. The times are simulated.
32 devices in a mesh: tile: 4 (over x, core), blk: 8 (over z, y).
Axes of the slice: x: 2, y: 2, z: 4, core: 2. Of those that a mesh axis runs over, the one named last changes fastest.
Arguments:
- tokens: bfloat16 [32768, 384], P(('tile', 'blk')), may hold values from -52 to 52
- ln_gain: float32 [384], replicated, may hold values from 0.1 to 1.9
- route: int32 [32768, 2], P(('tile', 'blk')), may hold values from 0 to 15, all different within a row; in each aligned block of 1024 rows (0 to 1023, 1024 to 2047, ...) at most 192 rows name the same one
- gates: float32 [32768, 2], P(('tile', 'blk')), may hold values from 0.1 to 1
- w_gate: bfloat16 [16, 384, 1024], P('tile', 'blk'), may hold values from -0.3125 to 0.3125
- w_up: bfloat16 [16, 384, 1024], P('tile', 'blk'), may hold values from -0.3125 to 0.3125
- w_down: bfloat16 [16, 1024, 384], P('tile', 'blk'), may hold values from -0.1875 to 0.1875
- d_mixed: bfloat16 [32768, 384], P(('tile', 'blk')), may hold values from -6 to 6
Outputs:
- mixed: bfloat16 [32768, 384], P(('tile', 'blk'))
- grad_gates: float32 [32768, 2], P(('tile', 'blk'))
- grad_tokens: bfloat16 [32768, 384], P(('tile', 'blk'))
- grad_w_gate: float32 [16, 384, 1024], P('tile', 'blk')
- grad_w_up: float32 [16, 384, 1024], P('tile', 'blk')
- grad_w_down: float32 [16, 1024, 384], P('tile', 'blk')
Inputs may be any that keep to these rules, and one draw needn't show every extreme that they name: `route`: each row names 2 different experts; within the rows of one device no expert is named more than 192 times, a bound that some block reaches.
All inputs are finite; a program needn't handle non-finite values.
Results may differ from a plain program's by a relative error of at most 0.014.
Values may be sent and summed in bfloat16 or wider, within the bound.
A program may use at most 192 MiB of HBM per device.

v0:
```python
import functools
import math

import jax
import jax.numpy as jnp
from jax import lax
from jax.experimental import pallas as pl
from jax.experimental.pallas import tpu as pltpu
from jax.sharding import PartitionSpec as P

F32 = jnp.float32
BF16 = jnp.bfloat16
MESH = pl.DeviceIdType.MESH


def ring_order(count):
    inner = max(d for d in range(1, math.isqrt(count) + 1) if count % d == 0)
    outer = count // inner
    walk = [row * inner for row in range(outer)]
    for step, row in enumerate(reversed(range(outer))):
        cols = list(range(1, inner))
        if step % 2:
            cols.reverse()
        walk += [row * inner + col for col in cols]
    return walk


def lookup(table, index):
    total = jnp.int32(0)
    for place, value in enumerate(table):
        total = total + jnp.where(index == place, jnp.int32(value), jnp.int32(0))
    return total


def matmul(left, right, dims):
    return lax.dot_general(left, right, (dims, ((), ())), preferred_element_type=F32)


class Later:
    def __init__(self, **parts):
        self.parts = parts

    def __getattr__(self, name):
        return getattr(pltpu.make_async_remote_copy(**self.parts), name)


def kernel(
    tiles, blks, per_tile, cap,
    tok, gain, route_t, gates_t, w_gate, w_up, w_down, dmix,
    mixed, grad_gates, grad_tok, out_gate, out_up, out_dn,
    wgu, wdn, xs, ds, xr, dr, yr, dyr, ggu, gdn, rgu, rdn, tmp, cols, slot_r,
    load_sem, ag_send, ag_recv, rs_send, rs_recv, go_send, go_recv, go_own,
    back_send, back_recv, back_own,
):
    rows, feats = tok.shape
    hid = w_gate.shape[2]
    experts = tiles * per_tile
    half = hid // 2
    deep = hid // blks
    t = lax.axis_index("tile")
    b = lax.axis_index("blk")
    walk = ring_order(blks)
    where_is = [walk.index(i) for i in range(blks)]
    pos = lookup(where_is, b)

    def at(place):
        return lookup(walk, lax.rem(place + 4 * blks, blks))

    ring = (at(pos + 1), at(pos - 1))
    signs = (1, -1)

    def peer(jj):
        return lax.rem(t + jj, tiles)

    def source(jj):
        return lax.rem(t - jj + tiles, tiles)

    loads = []
    for index, (src, dst) in enumerate(
        ((w_gate, wgu.at[:, 0, b]), (w_up, wgu.at[:, 1, b]), (w_down, wdn.at[:, b]))
    ):
        loads.append(pltpu.make_async_copy(src, dst, load_sem.at[index]))
        loads[-1].start()

    barrier = pltpu.get_barrier_semaphore()
    for place in ring:
        pl.semaphore_signal(barrier, inc=1, device_id=(t, place), device_id_type=MESH)
    for jj in range(1, tiles):
        pl.semaphore_signal(barrier, inc=1, device_id=(peer(jj), b), device_id_type=MESH)
    pl.semaphore_wait(barrier, 2 + tiles - 1)
    for load in loads:
        load.wait()

    def ag_copies(e, s, way):
        owner = at(pos - signs[way] * s)
        return [
            pltpu.make_async_remote_copy(
                src_ref=ref, dst_ref=ref,
                send_sem=ag_send.at[e, way, s, part], recv_sem=ag_recv.at[e, way, s, part],
                device_id=(t, ring[way]), device_id_type=MESH,
            )
            for part, ref in enumerate((wgu.at[e, :, owner], wdn.at[e, owner]))
        ]

    def ag_wait_copies(e, s, way):
        owner = at(pos - signs[way] * (s + 1))
        return [
            pltpu.make_async_remote_copy(
                src_ref=ref, dst_ref=ref,
                send_sem=ag_send.at[e, way, s, part], recv_sem=ag_recv.at[e, way, s, part],
                device_id=(t, ring[way]), device_id_type=MESH,
            )
            for part, ref in enumerate((wgu.at[e, :, owner], wdn.at[e, owner]))
        ]

    hops = blks // 2

    def ag_each(e, s, action):
        for way in range(2):
            @pl.when(jnp.logical_or(s < hops - 1, jnp.logical_and(s == hops - 1, lax.rem(e, 2) == way)))
            def _():
                action(e, s, way)

    def ag_start(e, s):
        def go(e, s, way):
            for copy in ag_copies(e, s, way):
                copy.start()
        ag_each(e, s, go)

    def ag_wait(e, s):
        def land(e, s, way):
            for copy in ag_wait_copies(e, s, way):
                copy.wait_recv()
        ag_each(e, s, land)

    def ag_sent(e, s):
        def done(e, s, way):
            for copy in ag_copies(e, s, way):
                copy.wait_send()
        ag_each(e, s, done)

    def rs_copies(e, s, way):
        chunk = at(pos - signs[way] * (s + 1))
        return [
            Later(
                src_ref=src, dst_ref=dst,
                send_sem=rs_send.at[e, way, s, part], recv_sem=rs_recv.at[e, way, s, part],
                device_id=(t, ring[way]), device_id_type=MESH,
            )
            for part, (src, dst) in enumerate((
                (ggu.at[e, way, chunk], rgu.at[e, way, s]),
                (gdn.at[e, way, chunk], rdn.at[e, way, s]),
            ))
        ]

    def rs_start(e, s):
        for way in range(2):
            for copy in rs_copies(e, s, way):
                copy.start()

    last = blks - 2

    def rs_step(e, s):
        for part, (own, landed) in enumerate(((ggu, rgu), (gdn, rdn))):
            for way in range(2):
                rs_copies(e, s, way)[part].wait_recv()
                chunk = at(pos - signs[way] * (s + 2))
                total = own[e, way, chunk].astype(F32) + landed[e, way, s].astype(F32)

                @pl.when(s < last)
                def _():
                    own[e, way, chunk] = total.astype(BF16)
                    rs_copies(e, s + 1, way)[part].start()

                @pl.when(s == last)
                def _():
                    if part:
                        out_dn[e, way * (deep // 2) : (way + 1) * (deep // 2), :] = total
                    else:
                        out_gate[e, :, way * half : (way + 1) * half] = total[0]
                        out_up[e, :, way * half : (way + 1) * half] = total[1]

    def row_copies(src, dst, send, recv, own, e, jj, part, place):
        def here():
            return pltpu.make_async_copy(src, dst, own.at[e, part])

        def there():
            return pltpu.make_async_remote_copy(
                src_ref=src, dst_ref=dst, send_sem=send.at[e, jj, part],
                recv_sem=recv.at[e, jj, part], device_id=(place, b), device_id_type=MESH,
            )

        return here, there

    def go_pairs(e, jj, at_tile):
        return [
            row_copies(src.at[e, jj], dst.at[e, at_tile], go_send, go_recv, go_own, e, jj, part, peer(jj))
            for part, (src, dst) in enumerate(((xs, xr), (ds, dr)))
        ]

    def back_pairs(e, jj, at_tile):
        return [
            row_copies(src.at[e, peer(jj)], dst.at[at_tile, e], back_send, back_recv, back_own, e, jj, part, peer(jj))
            for part, (src, dst) in enumerate(((xr, yr), (dr, dyr)))
        ]

    for e in range(min(2, per_tile)):
        ag_start(e, 0)

    block = min(256, rows)

    def slots(i, carry):
        base = pl.multiple_of(i * block, block)
        span = pl.ds(base, block)
        names = lax.broadcasted_iota(jnp.int32, (experts, rows), 0)
        count = (route_t[0:1, :] == names).astype(F32) + (route_t[1:2, :] == names).astype(F32)
        row = lax.broadcasted_iota(jnp.int32, (rows, block), 0)
        col = lax.broadcasted_iota(jnp.int32, (rows, block), 1) + base
        before = matmul(count.astype(BF16), (row < col).astype(F32).astype(BF16), ((1,), (0,)))
        part = route_t[:, span]
        name = lax.broadcasted_iota(jnp.int32, (experts, block), 0)
        line = lax.broadcasted_iota(jnp.int32, (8, block), 0)
        stack = jnp.zeros((8, block), F32)
        for k in range(2):
            mine = part[k : k + 1, :]
            rank = jnp.sum(jnp.where(mine == name, before, 0.0), axis=0, keepdims=True)
            slot = mine * cap + rank.astype(jnp.int32)
            slot_r[k : k + 1, span] = slot
            stack = jnp.where(line == k, slot.astype(F32), stack)
            stack = jnp.where(line == k + 2, gates_t[k : k + 1, span], stack)
        turned = stack.T
        cols[span, :] = turned
        x = tok[span, :].astype(F32)
        centred = x - jnp.mean(x, axis=-1, keepdims=True)
        spread = jnp.mean(centred * centred, axis=-1, keepdims=True)
        d = dmix[span, :].astype(F32)
        tmp[0, span, 0:feats] = (x * lax.rsqrt(spread + 1e-05) * gain[...]).astype(BF16)
        tmp[1, span, 0:feats] = (turned[:, 2:3] * d).astype(BF16)
        tmp[2, span, 0:feats] = (turned[:, 3:4] * d).astype(BF16)
        return carry

    lax.fori_loop(0, rows // block, slots, 0)

    def pack(i, carry):
        e, jj = i // tiles, lax.rem(i, tiles)
        dest = peer(jj)
        want = lax.broadcasted_iota(jnp.int32, (cap, rows), 0) + (dest * per_tile + e) * cap
        first = (slot_r[0:1, :] == want).astype(F32)
        second = (slot_r[1:2, :] == want).astype(F32)
        xs[e, jj] = matmul((first + second).astype(BF16), tmp[0, 0:rows, 0:feats], ((1,), (0,))).astype(BF16)
        ds[e, jj] = (
            matmul(first.astype(BF16), tmp[1, 0:rows, 0:feats], ((1,), (0,)))
            + matmul(second.astype(BF16), tmp[2, 0:rows, 0:feats], ((1,), (0,)))
        ).astype(BF16)

        @pl.when(jj == 0)
        def _():
            for here, there in go_pairs(e, jj, t):
                here().start()

        @pl.when(jj > 0)
        def _():
            for here, there in go_pairs(e, jj, t):
                there().start()

        @pl.when(jnp.logical_and(lax.rem(i, 4) == 3, i // 4 < hops))
        def _():
            ag_event(2 * (i // 4))
            ag_event(2 * (i // 4) + 1)

        return carry

    def ag_event(j):
        e = 2 * (j // (2 * hops)) + lax.rem(j, 2)
        s = lax.rem(j // 2, hops)
        ag_wait(e, s)

        @pl.when(s + 1 < hops)
        def _():
            ag_start(e, s + 1)

        @pl.when(jnp.logical_and(s == hops - 1, e + 2 < per_tile))
        def _():
            ag_start(e + 2, 0)

    lax.fori_loop(0, per_tile * tiles, pack, 0)

    def late(j, carry):
        ag_event(j)
        return carry

    lax.fori_loop(min(2 * hops, 2 * (per_tile * tiles // 4)), 2 * hops, late, 0)
    points = 2 * tiles

    def service_rs(e, k):
        old, young = points // 2 + k // 2, k // 2

        @pl.when(jnp.logical_and(jnp.logical_and(e >= 2, e - 2 < per_tile), jnp.logical_and(lax.rem(k, 2) == 0, old <= last)))
        def _():
            rs_step(e - 2, old)

        @pl.when(jnp.logical_and(jnp.logical_and(e >= 1, e - 1 < per_tile), jnp.logical_and(lax.rem(k, 2) == 1, young <= last)))
        def _():
            rs_step(e - 1, young)

    def service(e, k):
        j = 2 * hops + (e * points + k) // 2

        @pl.when(jnp.logical_and(lax.rem(k, 2) == 0, j < per_tile * hops))
        def _():
            ag_event(j)

        service_rs(e, k)

    def expert(e, carry):
        for jj in range(tiles):
            for here, there in go_pairs(e, jj, source(jj)):
                if jj == 0:
                    here().wait()
                else:
                    there().wait_recv()

        def forward(i, carry):
            span = pl.ds(pl.multiple_of(i * cap, cap), cap)
            x, d = xr[e, i], dr[e, i]
            wide = (feats, hid)
            gate_pre = matmul(x, wgu[e, 0].reshape(wide), ((1,), (0,)))
            up_pre = matmul(x, wgu[e, 1].reshape(wide), ((1,), (0,)))
            d_act = matmul(d, wdn[e].reshape(hid, feats), ((1,), (1,)))
            sigma = jax.nn.sigmoid(gate_pre)
            swish = gate_pre * sigma
            tmp[0, span, :] = (swish * up_pre).astype(BF16)
            tmp[1, span, :] = (d_act * up_pre * sigma * (1.0 + gate_pre * (1.0 - sigma))).astype(BF16)
            tmp[2, span, :] = (d_act * swish).astype(BF16)
            service(e, i)
            return carry

        lax.fori_loop(0, tiles, forward, 0)

        many = tiles * cap
        x_all = xr[e].reshape(many, feats)
        for part in range(2):
            for way in range(2):
                grad = matmul(x_all, tmp[1 + part, 0:many, way * half : (way + 1) * half], ((0,), (0,)))
                ggu[e, way, :, part] = grad.reshape(blks, feats // blks, half).astype(BF16)
        width = min(256, hid)

        def down(i, carry):
            span = pl.ds(pl.multiple_of(i * width, width), width)
            grad = matmul(tmp[0, 0:many, span], dr[e].reshape(many, feats), ((0,), (0,)))
            grad = grad.reshape(width // deep, 2, deep // 2, feats).astype(BF16)
            for c in range(width // deep):
                for way in range(2):
                    gdn[e, way, i * (width // deep) + c] = grad[c, way]
            return carry

        lax.fori_loop(0, hid // width, down, 0)
        rs_start(e, 0)

        def backward(ii, carry):
            jj = lax.rem(ii + 1, tiles)
            i = peer(jj)
            span = pl.ds(pl.multiple_of(i * cap, cap), cap)
            wide = (feats, hid)
            y = matmul(tmp[0, span, :], wdn[e].reshape(hid, feats), ((1,), (0,)))
            d_in = matmul(tmp[1, span, :], wgu[e, 0].reshape(wide), ((1,), (1,)))
            d_in = d_in + matmul(tmp[2, span, :], wgu[e, 1].reshape(wide), ((1,), (1,)))
            xr[e, i] = y.astype(BF16)
            dr[e, i] = d_in.astype(BF16)
            service(e, tiles + ii)

            @pl.when(jj == 0)
            def _():
                for here, there in back_pairs(e, jj, t):
                    here().start()

            @pl.when(jj > 0)
            def _():
                for here, there in back_pairs(e, jj, t):
                    there().start()

            return carry

        lax.fori_loop(0, tiles, backward, 0)
        return carry

    lax.fori_loop(0, per_tile, expert, 0)

    def returned(e, carry):
        for jj in range(tiles):
            for here, there in back_pairs(e, jj, source(jj)):
                if jj == 0:
                    here().wait()
                else:
                    there().wait_recv()
        return carry

    few = min(128, rows)

    def finish(i):
        base = pl.multiple_of(i * few, few)
        span = pl.ds(base, few)
        column = cols[span, :]
        every = experts * cap
        want = lax.broadcasted_iota(jnp.int32, (few, every), 1)
        first = (column[:, 0:1].astype(jnp.int32) == want).astype(F32)
        second = (column[:, 1:2].astype(jnp.int32) == want).astype(F32)
        y = yr[...].reshape(every, feats)
        y0 = matmul(first.astype(BF16), y, ((1,), (0,)))
        y1 = matmul(second.astype(BF16), y, ((1,), (0,)))
        dn = matmul((first + second).astype(BF16), dyr[...].reshape(every, feats), ((1,), (0,)))
        d = dmix[span, :].astype(F32)
        mixed[span, :] = (column[:, 2:3] * y0 + column[:, 3:4] * y1).astype(BF16)
        lane = lax.broadcasted_iota(jnp.int32, (few, 128), 1)
        dots = jnp.where(lane == 0, jnp.sum(d * y0, axis=-1, keepdims=True), 0.0)
        dots = jnp.where(lane == 1, jnp.sum(d * y1, axis=-1, keepdims=True), dots)
        grad_gates[:, span] = dots.T[0:2, :]
        x = tok[span, :].astype(F32)
        centred = x - jnp.mean(x, axis=-1, keepdims=True)
        spread = jnp.mean(centred * centred, axis=-1, keepdims=True)
        r = lax.rsqrt(spread + 1e-05)
        u = dn * gain[...]
        pull = jnp.sum(u * x, axis=-1, keepdims=True) * (r * r * r) / feats
        grad_tok[span, :] = (u * r - pull * centred).astype(BF16)

    begin = points // 2

    def tail(k, carry):
        service_rs(per_tile + k // points, lax.rem(k, points))

        @pl.when(k == begin)
        def _():
            lax.fori_loop(0, per_tile, returned, 0)

        @pl.when(jnp.logical_and(k >= begin, k < begin + rows // few))
        def _():
            finish(k - begin)

        return carry

    lax.fori_loop(0, max(2 * points, begin + rows // few), tail, 0)

    def drain(e, carry):
        def ag_done(s, carry):
            ag_sent(e, s)
            return carry

        lax.fori_loop(0, hops, ag_done, 0)

        def rs_done(s, carry):
            for way in range(2):
                for copy in rs_copies(e, s, way):
                    copy.wait_send()
            return carry

        lax.fori_loop(0, blks - 1, rs_done, 0)
        for jj in range(1, tiles):
            for here, there in go_pairs(e, jj, t) + back_pairs(e, jj, t):
                there().wait_send()
        return carry

    lax.fori_loop(0, per_tile, drain, 0)


def on_device(tiles, blks, tokens, ln_gain, route, gates, w_gate, w_up, w_down, d_mixed):
    rows, feats = tokens.shape
    per_tile, thin, hid = w_gate.shape
    deep = w_down.shape[1]
    experts = per_tile * tiles
    cap = max(2, 3 * rows * route.shape[1] // (2 * experts))
    half = hid // 2
    hops = blks // 2
    vmem = pl.BlockSpec(memory_space=pltpu.VMEM)
    hbm = pl.BlockSpec(memory_space=pl.ANY)
    moved = (per_tile, tiles, cap, feats)
    dma = pltpu.SemaphoreType.DMA
    outs = pl.pallas_call(
        functools.partial(kernel, tiles, blks, per_tile, cap),
        out_shape=(
            jax.ShapeDtypeStruct((rows, feats), BF16),
            jax.ShapeDtypeStruct((2, rows), F32),
            jax.ShapeDtypeStruct((rows, feats), BF16),
            jax.ShapeDtypeStruct((per_tile, thin, hid), F32),
            jax.ShapeDtypeStruct((per_tile, thin, hid), F32),
            jax.ShapeDtypeStruct((per_tile, deep, feats), F32),
        ),
        in_specs=[vmem, vmem, vmem, vmem, hbm, hbm, hbm, vmem],
        out_specs=[vmem] * 6,
        scratch_shapes=[
            pltpu.VMEM((per_tile, 2, blks, thin, hid), BF16),
            pltpu.VMEM((per_tile, blks, deep, feats), BF16),
            pltpu.VMEM(moved, BF16),
            pltpu.VMEM(moved, BF16),
            pltpu.VMEM(moved, BF16),
            pltpu.VMEM(moved, BF16),
            pltpu.VMEM((tiles, per_tile, cap, feats), BF16),
            pltpu.VMEM((tiles, per_tile, cap, feats), BF16),
            pltpu.VMEM((per_tile, 2, blks, 2, thin, half), BF16),
            pltpu.VMEM((per_tile, 2, blks, deep // 2, feats), BF16),
            pltpu.VMEM((per_tile, 2, blks - 1, 2, thin, half), BF16),
            pltpu.VMEM((per_tile, 2, blks - 1, deep // 2, feats), BF16),
            pltpu.VMEM((3, max(rows, tiles * cap), max(hid, feats)), BF16),
            pltpu.VMEM((rows, 8), F32),
            pltpu.VMEM((2, rows), jnp.int32),
            dma((3,)),
            dma((per_tile, 2, hops, 2)),
            dma((per_tile, 2, hops, 2)),
            dma((per_tile, 2, blks - 1, 2)),
            dma((per_tile, 2, blks - 1, 2)),
            dma((per_tile, tiles, 2)),
            dma((per_tile, tiles, 2)),
            dma((per_tile, 2)),
            dma((per_tile, tiles, 2)),
            dma((per_tile, tiles, 2)),
            dma((per_tile, 2)),
        ],
        compiler_params=pltpu.CompilerParams(
            collective_id=0, has_side_effects=True, vmem_limit_bytes=67043328
        ),
    )(tokens, ln_gain.reshape(1, feats), route.T, gates.T, w_gate, w_up, w_down, d_mixed)
    return (outs[0], outs[1].T) + tuple(outs[2:])


def solution(mesh):
    rows_spec = P(("tile", "blk"), None)
    weight_spec = P("tile", "blk", None)
    return jax.shard_map(
        functools.partial(on_device, mesh.shape["tile"], mesh.shape["blk"]),
        mesh=mesh,
        in_specs=(rows_spec, P(), rows_spec, rows_spec) + (weight_spec,) * 3 + (rows_spec,),
        out_specs=(rows_spec,) * 3 + (weight_spec,) * 3,
        check_vma=False,
    )
```

profile of v0, /device:TPU:0, one launch (start us, length us, event | category | flops | bytes accessed | tf_op | source)
XLA Modules:
  0.0 214.3 jit_solution(2443851505164798478)
XLA Ops:
  0.6 0.0 copy-start.5
  0.6 0.7 copy-done.5
  1.3 0.6 reshape.15.gain
  1.9 204.5 %shard_map.127 = (bf16[1024,384]{1,0:T(8,128)(2,1)}, f32[2,1024]{1,0:T(2,128)}, bf16[1024,384]{1,0:T(8,128)(2,1)}, f32[4,48,1024]{2,1,0:T(8,128)}, f32[4,48,1024]{2,1,0:T(8,128)}, /*index=5*/f32[4,128,384]{2,1,0:T(8,128)}) custom-call(bf16[1024,384]{1,0:T(8,128)(2,1)} %tok.1, f32[1,384]{1,0:T(1,128)} %reshape.15.gain, s32[2,1024]{1,0:T(2,128)} %bitcast.3, ...), custom_call_target="tpu_custom_call" | custom-call | tf_op jit(solution)/shard_map/pallas_call | solution.py:477
  206.4 0.0 copy-start.4
  206.4 0.0 copy-start.3
  206.4 2.2 %copy.20 = bf16[1024,384]{1,0:T(8,128)(2,1)} copy(bf16[1024,384]{1,0:T(8,128)(2,1)} %get-tuple-element.24) | data formatting | bytes 1572864
  208.5 0.0 copy-done.4
  208.5 0.6 copy.21
  209.1 0.0 copy-done.3
  209.1 0.0 copy-start.2
  209.2 0.9 copy.22
  210.0 0.5 copy-done.2
  210.6 0.0 copy-start.1
  210.6 0.9 copy.23
  211.4 0.5 copy-done.1
  212.0 0.0 copy-start
  212.0 0.9 copy.24
  212.9 0.5 copy-done
  213.4 0.9 copy.25
Async XLA Ops:
  0.6 0.7 copy-start.5
  206.4 2.2 %copy-start.4 = (f32[2,1024]{1,0:T(2,128)S(1)}, f32[2,1024]{1,0:T(2,128)}, u32[]{:S(2)}) copy-start(f32[2,1024]{1,0:T(2,128)} %get-tuple-element.13) | copy-start | bytes 24580
  206.4 2.8 %copy-start.3 = (bf16[1024,384]{1,0:T(8,128)(2,1)S(1)}, bf16[1024,384]{1,0:T(8,128)(2,1)}, u32[]{:S(2)}) copy-start(bf16[1024,384]{1,0:T(8,128)(2,1)} %get-tuple-element.26) | copy-start | bytes 2359300
  209.1 1.4 copy-start.2
  210.6 1.4 copy-start.1
  212.0 1.4 copy-start
where the time goes:
time: 215 us; the launch traced here: 214 us
  Pallas kernels  204 us (95%)
  local copies, waits for them, and re-layouts  9.14 us (4%)
    pallas_call x1, Pallas kernels, on_device(): pl.pallas_call(functools.partial(kernel, tiles, blks, per_tile, cap), out...  204 us
    unnamed x18, local copies, waits for them, and re-layouts  8.57 us

commit v1 on v0

v1 whole, which is shorter than its diff:
```python
import functools
import math

import jax
import jax.numpy as jnp
from jax import lax
from jax.experimental import pallas as pl
from jax.experimental.pallas import tpu as pltpu
from jax.sharding import PartitionSpec as P

F32 = jnp.float32
BF16 = jnp.bfloat16
MESH = pl.DeviceIdType.MESH


def matmul(left, right, dims=((1,), (0,))):
    return lax.dot_general(left, right, (dims, ((), ())), preferred_element_type=F32)


def onehot(mask):
    return mask.astype(F32).astype(BF16)


def both(*conditions):
    total = conditions[0]
    for condition in conditions[1:]:
        total = jnp.logical_and(total, condition)
    return total


def kernel(
    tiles, inner, outer, per_dev, cap,
    tok, gain, route_t, gates_t, w_gate, w_up, w_down, dmix,
    mixed, grad_gates, grad_tok, out_gate, out_up, out_dn,
    wgu, wdn, xs, xr, yr, ggu, gdn, rgu, rdn, fgu, fdn, tgu, tdn, prep, tmp, acc, cols, slot_r,
    load_sem, sw_send, sw_recv, ag_send, ag_recv, rs_send, rs_recv, fs_send, fs_recv,
    go_send, go_recv, go_own, back_send, back_recv, back_own,
):
    rows, feats = tok.shape
    hid = w_gate.shape[2]
    blks = inner * outer
    thin, deep = feats // blks, hid // blks
    half = hid // 2
    group = tiles * inner
    wide = inner * cap
    many = tiles * wide
    t = lax.axis_index("tile")
    b = lax.axis_index("blk")
    r = b // inner
    y = lax.rem(b, inner)
    order = (0, 2, 1)

    def device(tile, row, col):
        return dict(device_id=(tile, row * inner + col), device_id_type=MESH)

    def shards(part, name):
        if part == 2:
            return (w_down.at[name],)
        span = slice(part * half, (part + 1) * half)
        return (w_gate.at[name, :, span], w_up.at[name, :, span])

    def places(part, e, blk):
        if part == 2:
            return (wdn.at[e, blk],)
        return (wgu.at[e, part, 0, blk], wgu.at[e, part, 1, blk])

    def loads(part, e):
        return [
            pltpu.make_async_copy(src, dst, load_sem.at[e, part, i])
            for i, (src, dst) in enumerate(zip(shards(part, y * per_dev + e), places(part, e, b)))
        ]

    def swaps(part, e, col, blk, mark):
        return [
            pltpu.make_async_remote_copy(
                src_ref=src, dst_ref=dst, send_sem=sw_send.at[e, part, col, i],
                recv_sem=sw_recv.at[e, part, mark, i], **device(t, r, col),
            )
            for i, (src, dst) in enumerate(zip(shards(part, col * per_dev + e), places(part, e, blk)))
        ]

    def other_columns(action):
        for col in range(inner):
            pl.when(col != y)(functools.partial(action, col))

    def swap_start(e):
        for part in order:
            def go(col):
                for copy in swaps(part, e, col, b, y):
                    copy.start()
            other_columns(go)

    def weight_rows(part, e, row):
        span = pl.ds(row * inner, inner)
        return wdn.at[e, span] if part == 2 else wgu.at[e, part, :, span]

    def ag_copy(part, e, way, s, row):
        ref = weight_rows(part, e, row)
        return pltpu.make_async_remote_copy(
            src_ref=ref, dst_ref=ref, send_sem=ag_send.at[e, part, way, s],
            recv_sem=ag_recv.at[e, part, way, s], **device(t, r - 1 if way else r + 1, y),
        )

    def ag_has(way, s):
        return both(r >= 1, r + s < outer) if way else both(r + 1 < outer, r - s >= 0)

    def ag_sent_row(way, s):
        return r + s if way else r - s

    def ag_own(part, e):
        for copy in loads(part, e):
            copy.wait()

        def land(col):
            for copy in swaps(part, e, col, r * inner + col, col):
                copy.wait_recv()
        other_columns(land)
        for way in range(2):
            @pl.when(ag_has(way, 0))
            def _():
                ag_copy(part, e, way, 0, r).start()

    def ag_event(part, e, s):
        for way in range(2):
            row = r + 1 + s if way else r - 1 - s

            @pl.when(row < outer if way else row >= 0)
            def _():
                ag_copy(part, e, way, s, row).wait_recv()
                if s + 1 < outer - 1:
                    @pl.when(r >= 1 if way else r + 1 < outer)
                    def _():
                        ag_copy(part, e, way, s + 1, row).start()

    def grad_rows(part, e, row):
        span = pl.ds(row * inner, inner)
        return gdn.at[e, span] if part == 2 else ggu.at[e, part, :, span]

    def landed(part, e, way, k):
        return rdn.at[e, way, k] if part == 2 else rgu.at[e, part, way, k]

    def rs_copy(part, e, way, k):
        return pltpu.make_async_remote_copy(
            src_ref=grad_rows(part, e, k if way else outer - 1 - k), dst_ref=landed(part, e, way, k),
            send_sem=rs_send.at[e, part, way, k], recv_sem=rs_recv.at[e, part, way, k],
            **device(t, r - 1 if way else r + 1, y),
        )

    def fs_copy(part, e, col, mark):
        if part == 2:
            src, dst = gdn.at[e, r * inner + col], fdn.at[e, mark]
        else:
            src, dst = ggu.at[e, part, :, r * inner + col], fgu.at[e, part, mark]
        return pltpu.make_async_remote_copy(
            src_ref=src, dst_ref=dst, send_sem=fs_send.at[e, part, col],
            recv_sem=fs_recv.at[e, part, mark], **device(t, r, col),
        )

    def put(part, name, value):
        if part == 2:
            out_dn[name] = value
        else:
            span = slice(part * half, (part + 1) * half)
            out_gate[name, :, span] = value[0]
            out_up[name, :, span] = value[1]

    def rs_start(part, e):
        for way in range(2):
            far = outer - 1 - r if way else r

            @pl.when(far == 0)
            def _():
                for k in range(outer - 1):
                    rs_copy(part, e, way, k).start()

    def rs_event(part, e, step):
        for way in range(2):
            far = outer - 1 - r if way else r

            @pl.when(both(far > 0, far <= step))
            def _():
                k = step - far
                own, new = grad_rows(part, e, k if way else outer - 1 - k), landed(part, e, way, k)
                rs_copy(part, e, way, k).wait_recv()
                own[...] = (own[...].astype(F32) + new[...].astype(F32)).astype(BF16)
                rs_copy(part, e, way, k).start()

    def rs_final(part, e):
        total = tdn if part == 2 else tgu
        total[...] = grad_rows(part, e, r)[...].astype(F32)
        for way in range(2):
            far = outer - 1 - r if way else r

            @pl.when(far > 0)
            def _():
                k = outer - 1 - far
                rs_copy(part, e, way, k).wait_recv()
                total[...] += landed(part, e, way, k)[...].astype(F32)

        for col in range(inner):
            value = total[col] if part == 2 else total[:, col]

            @pl.when(col == y)
            def _():
                put(part, col * per_dev + e, value)

            @pl.when(col != y)
            def _():
                if part == 2:
                    gdn[e, r * inner + col] = value.astype(BF16)
                else:
                    ggu[e, part, :, r * inner + col] = value.astype(BF16)
                fs_copy(part, e, col, y).start()

    def rs_take(part, e):
        def take(col):
            fs_copy(part, e, col, col).wait_recv()
            put(part, col * per_dev + e, (fdn[e, col] if part == 2 else fgu[e, part, col]).astype(F32))
        other_columns(take)

    def exchange(e, jt, action, backward, mark):
        tile = lax.rem(t + jt, tiles)
        from_tile = lax.rem(t - jt + tiles, tiles)
        for col in range(inner):
            if backward:
                src, dst = xr.at[e, tile, col], yr.at[e, t, y]
                landing = yr.at[e, from_tile, col]
                sems = back_send, back_recv, back_own
            else:
                src, dst = xs.at[e, jt, col], xr.at[e, t, y]
                landing = xr.at[e, from_tile, col]
                sems = go_send, go_recv, go_own

            def here():
                return pltpu.make_async_copy(src, dst, sems[2].at[e])

            def there():
                return pltpu.make_async_remote_copy(
                    src_ref=src, dst_ref=landing if mark else dst,
                    send_sem=sems[0].at[e, jt, col], recv_sem=sems[1].at[e, jt, col if mark else y],
                    **device(tile, r, col),
                )

            mine = both(jt == 0, col == y)
            pl.when(mine)(lambda: action(here(), True))
            pl.when(jnp.logical_not(mine))(lambda: action(there(), False))

    def begin(copy, local):
        copy.start()

    def arrive(copy, local):
        if local:
            copy.wait()
        else:
            copy.wait_recv()

    def leave(copy, local):
        if not local:
            copy.wait_send()

    def everywhere(e, action, backward, mark):
        def one(jt, carry):
            exchange(e, jt, action, backward, mark)
            return carry
        lax.fori_loop(0, tiles, one, 0)

    def service(i, *lists):
        for events in lists:
            for place, event in events:
                pl.when(i == place)(event)

    def spread(count, makers):
        return [(min(i, count - 1), maker) for i, maker in enumerate(makers)]

    for e in range(per_dev):
        for part in order:
            for copy in loads(part, e):
                copy.start()

    barrier = pltpu.get_barrier_semaphore()
    for jt in range(tiles):
        for col in range(inner):
            @pl.when(jnp.logical_or(jt > 0, col != y))
            def _():
                pl.semaphore_signal(barrier, inc=1, **device(lax.rem(t + jt, tiles), r, col))

    @pl.when(r > 0)
    def _():
        pl.semaphore_signal(barrier, inc=1, **device(t, r - 1, y))

    @pl.when(r + 1 < outer)
    def _():
        pl.semaphore_signal(barrier, inc=1, **device(t, r + 1, y))

    pl.semaphore_wait(
        barrier, group - 1 + jnp.where(r > 0, 1, 0) + jnp.where(r + 1 < outer, 1, 0)
    )
    swap_start(0)

    block = min(256, rows)
    blocks = rows // block

    def slots(i, carry):
        base = pl.multiple_of(i * block, block)
        span = pl.ds(base, block)
        experts = group * per_dev
        names = lax.broadcasted_iota(jnp.int32, (experts, rows), 0)
        count = (route_t[0:1, :] == names).astype(F32) + (route_t[1:2, :] == names).astype(F32)
        row = lax.broadcasted_iota(jnp.int32, (rows, block), 0)
        col = lax.broadcasted_iota(jnp.int32, (rows, block), 1) + base
        before = matmul(count.astype(BF16), onehot(row < col))
        part = route_t[:, span]
        name = lax.broadcasted_iota(jnp.int32, (experts, block), 0)
        line = lax.broadcasted_iota(jnp.int32, (8, block), 0)
        stack = jnp.zeros((8, block), F32)
        for k in range(2):
            mine = part[k : k + 1, :]
            rank = jnp.sum(jnp.where(mine == name, before, 0.0), axis=0, keepdims=True)
            owner = jnp.zeros_like(mine)
            for q in range(1, group):
                owner = owner + (mine >= q * per_dev).astype(jnp.int32)
            place = (mine - owner * per_dev) * group + owner
            slot = place * cap + rank.astype(jnp.int32)
            slot_r[k : k + 1, span] = slot
            stack = jnp.where(line == k, slot.astype(F32), stack)
            stack = jnp.where(line == k + 2, gates_t[k : k + 1, span], stack)
        cols[span, :] = stack.T
        x = tok[span, :].astype(F32)
        centred = x - jnp.mean(x, axis=-1, keepdims=True)
        spread_of = jnp.mean(centred * centred, axis=-1, keepdims=True)
        prep[span, 0:feats] = (x * lax.rsqrt(spread_of + 1e-05) * gain[...]).astype(BF16)
        prep[span, feats : 2 * feats] = dmix[span, :]
        service(i, [
            (min(1, blocks - 1), lambda: ag_own(0, 0)),
            (blocks - 1, lambda: ag_own(2, 0)),
        ])
        return carry

    lax.fori_loop(0, blocks, slots, 0)
    packs = per_dev * tiles

    def pack(i, carry):
        e, jt = i // tiles, lax.rem(i, tiles)
        dest = lax.rem(t + jt, tiles)
        want = lax.broadcasted_iota(jnp.int32, (wide, rows), 0) + (e * group + dest * inner) * cap
        first = slot_r[0:1, :] == want
        second = slot_r[1:2, :] == want
        weight = jnp.where(first, gates_t[0:1, :], jnp.where(second, gates_t[1:2, :], 0.0))
        scale = jnp.sum(weight, axis=1, keepdims=True)
        got = matmul(onehot(jnp.logical_or(first, second)), prep[...])
        xs[e, jt, :, :, 0:feats] = got[:, 0:feats].astype(BF16).reshape(inner, cap, feats)
        xs[e, jt, :, :, feats : 2 * feats] = (
            (scale * got[:, feats : 2 * feats]).astype(BF16).reshape(inner, cap, feats)
        )
        exchange(e, jt, begin, False, False)

        @pl.when(both(jt == tiles - 1, e + 1 < per_dev))
        def _():
            swap_start(e + 1)

        events = []
        for s in range(outer - 1):
            events.append((min(2 * s + 1, packs - 1), functools.partial(ag_event, 0, 0, s)))
            if s == min(1, outer - 2):
                events.append((min(2 * s + 1, packs - 1), lambda: ag_own(1, 0)))
            events.append((min(2 * s + 2, packs - 1), functools.partial(ag_event, 2, 0, s)))
        service(i, events)
        return carry

    lax.fori_loop(0, packs, pack, 0)

    def later(condition, event):
        return lambda: pl.when(condition)(event)

    def inputs(e, i):
        return xr[e, i, :, :, 0:feats].reshape(wide, feats), xr[e, i, :, :, feats : 2 * feats].reshape(wide, feats)

    def expert(e, carry):
        more = e + 1 < per_dev
        before = e >= 1

        def forward(h, events):
            span_h = slice(h * half, (h + 1) * half)
            deeper = blks // 2

            def one(i, carry):
                span = pl.ds(pl.multiple_of(i * wide, wide), wide)
                x, d = inputs(e, i)
                gate_pre = matmul(x, wgu[e, h, 0].reshape(feats, half))
                up_pre = matmul(x, wgu[e, h, 1].reshape(feats, half))
                down = wdn[e, h * deeper : (h + 1) * deeper].reshape(half, feats)
                d_act = matmul(d, down, ((1,), (1,)))
                sigma = jax.nn.sigmoid(gate_pre)
                swish = gate_pre * sigma
                tmp[0, span, span_h] = (swish * up_pre).astype(BF16)
                tmp[1, span, span_h] = (d_act * up_pre * sigma * (1.0 + gate_pre * (1.0 - sigma))).astype(BF16)
                tmp[2, span, span_h] = (d_act * swish).astype(BF16)
                service(i, *events)
                return carry

            lax.fori_loop(0, tiles, one, 0)

        def grads(h):
            x_all = xr[e, :, :, :, 0:feats].reshape(many, feats)
            for g in range(2):
                grad = matmul(x_all, tmp[1 + g, :, h * half : (h + 1) * half], ((0,), (0,)))
                ggu[e, h, g] = grad.astype(BF16).reshape(blks, thin, half)

        width = min(256, hid)

        def downs(i, carry):
            span = pl.ds(pl.multiple_of(i * width, width), width)
            d_all = xr[e, :, :, :, feats : 2 * feats].reshape(many, feats)
            grad = matmul(tmp[0, :, span], d_all, ((0,), (0,)))
            count = width // deep
            gdn[e, pl.ds(i * count, count)] = grad.astype(BF16).reshape(count, deep, feats)
            return carry

        def back(ii, carry):
            jt = lax.rem(ii + 1, tiles)
            i = lax.rem(t + jt, tiles)
            span = pl.ds(pl.multiple_of(i * wide, wide), wide)
            out = matmul(tmp[0, span, :], wdn[e].reshape(hid, feats))
            d_in = jnp.zeros((wide, feats), F32)
            for h in range(2):
                for g in range(2):
                    d_in = d_in + matmul(
                        tmp[1 + g, span, h * half : (h + 1) * half],
                        wgu[e, h, g].reshape(feats, half), ((1,), (1,)),
                    )
            xr[e, i, :, :, 0:feats] = out.astype(BF16).reshape(inner, cap, feats)
            xr[e, i, :, :, feats : 2 * feats] = d_in.astype(BF16).reshape(inner, cap, feats)
            exchange(e, jt, begin, True, False)
            service(ii, *back_events)
            return carry

        def ags(part, e, condition=None):
            events = [functools.partial(ag_event, part, e, s) for s in range(outer - 1)]
            if condition is not None:
                events = [later(condition, event) for event in events]
            return spread(tiles, events)

        everywhere(e, arrive, False, True)

        @pl.when(more)
        def _():
            ag_own(0, e + 1)

        tails = [later(before, event) for event in tail_events(e - 1)]
        forward(0, [ags(1, e), spread(tiles, tails)])
        grads(0)
        rs_start(0, e)

        @pl.when(more)
        def _():
            ag_own(2, e + 1)

        steps = [functools.partial(rs_event, 0, e, step) for step in range(1, outer - 1)]
        forward(1, [
            ags(0, e + 1, more),
            [(min(2 * i + 1, tiles - 1), event) for i, event in enumerate(steps)],
        ])
        grads(1)
        rs_start(1, e)
        lax.fori_loop(0, hid // width, downs, 0)
        rs_start(2, e)
        rs_final(0, e)

        @pl.when(more)
        def _():
            ag_own(1, e + 1)

        steps = []
        for step in range(1, outer - 1):
            steps += [functools.partial(rs_event, 1, e, step), functools.partial(rs_event, 2, e, step)]
        back_events = [ags(2, e + 1, more), spread(tiles, steps), [(tiles - 1, lambda: rs_take(0, e))]]
        lax.fori_loop(0, tiles, back, 0)
        return carry

    def tail_events(e):
        return [
            functools.partial(rs_final, 1, e), functools.partial(rs_final, 2, e),
            functools.partial(rs_take, 1, e), functools.partial(rs_take, 2, e),
        ]

    lax.fori_loop(0, per_dev, expert, 0)

    few = min(256, rows)

    def gather(i, e):
        span = pl.ds(pl.multiple_of(i * few, few), few)
        column = cols[span, :]
        want = lax.broadcasted_iota(jnp.int32, (few, many), 1) + e * many
        first = onehot(column[:, 0:1].astype(jnp.int32) == want)
        second = onehot(column[:, 1:2].astype(jnp.int32) == want)
        value = yr[e].reshape(many, 2 * feats)
        y0 = matmul(first, value[:, 0:feats])
        y1 = matmul(second, value[:, 0:feats])
        dn = matmul(first + second, value[:, feats : 2 * feats])
        return span, column, y0, y1, dn

    def early(e, carry):
        everywhere(e, arrive, True, True)

        def one(i, carry):
            span, column, y0, y1, dn = gather(i, e)
            for k, value in enumerate((y0, y1, dn)):
                lanes = slice(k * feats, (k + 1) * feats)
                old = jnp.where(e == 0, 0.0, acc[span, lanes])
                acc[span, lanes] = old + value
            return carry

        lax.fori_loop(0, rows // few, one, 0)
        return carry

    lax.fori_loop(0, per_dev - 1, early, 0)
    last = per_dev - 1
    ending = tail_events(last)
    ending[0]()
    ending[1]()
    everywhere(last, arrive, True, True)

    def finish(i, carry):
        span, column, y0, y1, dn = gather(i, last)
        if last:
            y0, y1, dn = [
                value + acc[span, k * feats : (k + 1) * feats] for k, value in enumerate((y0, y1, dn))
            ]
        d = dmix[span, :].astype(F32)
        mixed[span, :] = (column[:, 2:3] * y0 + column[:, 3:4] * y1).astype(BF16)
        lane = lax.broadcasted_iota(jnp.int32, (few, 128), 1)
        dots = jnp.where(lane == 0, jnp.sum(d * y0, axis=-1, keepdims=True), 0.0)
        dots = jnp.where(lane == 1, jnp.sum(d * y1, axis=-1, keepdims=True), dots)
        grad_gates[:, span] = dots.T[0:2, :]
        x = tok[span, :].astype(F32)
        centred = x - jnp.mean(x, axis=-1, keepdims=True)
        spread_of = jnp.mean(centred * centred, axis=-1, keepdims=True)
        scale = lax.rsqrt(spread_of + 1e-05)
        u = dn * gain[...]
        pull = jnp.sum(u * x, axis=-1, keepdims=True) * (scale * scale * scale) / feats
        grad_tok[span, :] = (u * scale - pull * centred).astype(BF16)
        return carry

    lax.fori_loop(0, rows // few, finish, 0)
    ending[2]()
    ending[3]()

    def drain(e, carry):
        everywhere(e, leave, False, False)
        everywhere(e, leave, True, False)
        for part in range(3):
            def sent(col):
                for copy in swaps(part, e, col, b, y):
                    copy.wait_send()
                fs_copy(part, e, col, y).wait_send()
            other_columns(sent)
            for way in range(2):
                far = outer - 1 - r if way else r
                for s in range(outer - 1):
                    @pl.when(ag_has(way, s))
                    def _():
                        ag_copy(part, e, way, s, ag_sent_row(way, s)).wait_send()

                    @pl.when(far + s < outer - 1)
                    def _():
                        rs_copy(part, e, way, s).wait_send()
        return carry

    lax.fori_loop(0, per_dev, drain, 0)


def on_device(tiles, blks, tokens, ln_gain, route, gates, w_gate, w_up, w_down, d_mixed):
    rows, feats = tokens.shape
    per_tile, thin, hid = w_gate.shape
    deep = w_down.shape[1]
    experts = per_tile * tiles
    cap = max(2, 3 * rows * route.shape[1] // (2 * experts))
    half = hid // 2
    inner = max(d for d in range(1, math.isqrt(blks) + 1) if blks % d == 0)
    outer = blks // inner
    per_dev = per_tile // inner
    many = tiles * inner * cap
    vmem = pl.BlockSpec(memory_space=pltpu.VMEM)
    hbm = pl.BlockSpec(memory_space=pl.ANY)
    dma = pltpu.SemaphoreType.DMA
    outs = pl.pallas_call(
        functools.partial(kernel, tiles, inner, outer, per_dev, cap),
        out_shape=(
            jax.ShapeDtypeStruct((rows, feats), BF16),
            jax.ShapeDtypeStruct((2, rows), F32),
            jax.ShapeDtypeStruct((rows, feats), BF16),
            jax.ShapeDtypeStruct((per_tile, thin, hid), F32),
            jax.ShapeDtypeStruct((per_tile, thin, hid), F32),
            jax.ShapeDtypeStruct((per_tile, deep, feats), F32),
        ),
        in_specs=[vmem, vmem, vmem, vmem, hbm, hbm, hbm, vmem],
        out_specs=[vmem] * 6,
        scratch_shapes=[
            pltpu.VMEM((per_dev, 2, 2, blks, thin, half), BF16),
            pltpu.VMEM((per_dev, blks, deep, feats), BF16),
            pltpu.VMEM((per_dev, tiles, inner, cap, 2 * feats), BF16),
            pltpu.VMEM((per_dev, tiles, inner, cap, 2 * feats), BF16),
            pltpu.VMEM((per_dev, tiles, inner, cap, 2 * feats), BF16),
            pltpu.VMEM((per_dev, 2, 2, blks, thin, half), BF16),
            pltpu.VMEM((per_dev, blks, deep, feats), BF16),
            pltpu.VMEM((per_dev, 2, 2, outer - 1, 2, inner, thin, half), BF16),
            pltpu.VMEM((per_dev, 2, outer - 1, inner, deep, feats), BF16),
            pltpu.VMEM((per_dev, 2, inner, 2, thin, half), BF16),
            pltpu.VMEM((per_dev, inner, deep, feats), BF16),
            pltpu.VMEM((2, inner, thin, half), F32),
            pltpu.VMEM((inner, deep, feats), F32),
            pltpu.VMEM((rows, 2 * feats), BF16),
            pltpu.VMEM((3, many, hid), BF16),
            pltpu.VMEM((rows if per_dev > 1 else 8, 3 * feats), F32),
            pltpu.VMEM((rows, 8), F32),
            pltpu.VMEM((2, rows), jnp.int32),
            dma((per_dev, 3, 2)),
            dma((per_dev, 3, inner, 2)),
            dma((per_dev, 3, inner, 2)),
            dma((per_dev, 3, 2, outer - 1)),
            dma((per_dev, 3, 2, outer - 1)),
            dma((per_dev, 3, 2, outer - 1)),
            dma((per_dev, 3, 2, outer - 1)),
            dma((per_dev, 3, inner)),
            dma((per_dev, 3, inner)),
            dma((per_dev, tiles, inner)),
            dma((per_dev, tiles, inner)),
            dma((per_dev,)),
            dma((per_dev, tiles, inner)),
            dma((per_dev, tiles, inner)),
            dma((per_dev,)),
        ],
        compiler_params=pltpu.CompilerParams(
            collective_id=0, has_side_effects=True, vmem_limit_bytes=67043328
        ),
    )(tokens, ln_gain.reshape(1, feats), route.T, gates.T, w_gate, w_up, w_down, d_mixed)
    return (outs[0], outs[1].T) + tuple(outs[2:])


def solution(mesh):
    rows_spec = P(("tile", "blk"), None)
    weight_spec = P("tile", "blk", None)
    return jax.shard_map(
        functools.partial(on_device, mesh.shape["tile"], mesh.shape["blk"]),
        mesh=mesh,
        in_specs=(rows_spec, P(), rows_spec, rows_spec) + (weight_spec,) * 3 + (rows_spec,),
        out_specs=(rows_spec,) * 3 + (weight_spec,) * 3,
        check_vma=False,
    )
```

time: 215 us -> 185 us (0.86)
  Pallas kernels: 204 us -> 175 us
    pallas_call x1, Pallas kernels: 204 us -> 175 us  [on_device(): pl.pallas_call(functools.partial(kernel, tiles, inner, outer, per_dev, ca...]
where the time goes in v1:
time: 185 us
  Pallas kernels  175 us (95%)
  local copies, waits for them, and re-layouts  9.14 us (5%)
    pallas_call x1, Pallas kernels, on_device(): pl.pallas_call(functools.partial(kernel, tiles, inner, outer, per_dev, ca...  175 us
    unnamed x18, local copies, waits for them, and re-layouts  8.57 us

profile of v1, /device:TPU:0, one launch (start us, length us, event | category | flops | bytes accessed | tf_op | source)
XLA Modules:
  0.0 184.6 jit_solution(18232416185928150040)
XLA Ops:
  0.6 0.0 copy-start.5
  0.6 0.7 copy-done.5
  1.3 0.6 reshape.15.gain
  1.9 174.8 %shard_map.127 = (bf16[1024,384]{1,0:T(8,128)(2,1)}, f32[2,1024]{1,0:T(2,128)}, bf16[1024,384]{1,0:T(8,128)(2,1)}, f32[4,48,1024]{2,1,0:T(8,128)}, f32[4,48,1024]{2,1,0:T(8,128)}, /*index=5*/f32[4,128,384]{2,1,0:T(8,128)}) custom-call(bf16[1024,384]{1,0:T(8,128)(2,1)} %tok.1, f32[1,384]{1,0:T(1,128)} %reshape.15.gain, s32[2,1024]{1,0:T(2,128)} %bitcast.3, ...), custom_call_target="tpu_custom_call" | custom-call | tf_op jit(solution)/shard_map/pallas_call | solution.py:586
  176.7 0.0 copy-start.4
  176.7 0.0 copy-start.3
  176.7 2.2 %copy.20 = bf16[1024,384]{1,0:T(8,128)(2,1)} copy(bf16[1024,384]{1,0:T(8,128)(2,1)} %get-tuple-element.24) | data formatting | bytes 1572864
  178.9 0.0 copy-done.4
  178.9 0.6 copy.21
  179.5 0.0 copy-done.3
  179.5 0.0 copy-start.2
  179.5 0.9 copy.22
  180.3 0.5 copy-done.2
  180.9 0.0 copy-start.1
  180.9 0.9 copy.23
  181.8 0.5 copy-done.1
  182.3 0.0 copy-start
  182.3 0.9 copy.24
  183.2 0.5 copy-done
  183.7 0.9 copy.25
Async XLA Ops:
  0.6 0.7 copy-start.5
  176.7 2.2 %copy-start.4 = (f32[2,1024]{1,0:T(2,128)S(1)}, f32[2,1024]{1,0:T(2,128)}, u32[]{:S(2)}) copy-start(f32[2,1024]{1,0:T(2,128)} %get-tuple-element.13) | copy-start | bytes 24580
  176.7 2.8 %copy-start.3 = (bf16[1024,384]{1,0:T(8,128)(2,1)S(1)}, bf16[1024,384]{1,0:T(8,128)(2,1)}, u32[]{:S(2)}) copy-start(bf16[1024,384]{1,0:T(8,128)(2,1)} %get-tuple-element.26) | copy-start | bytes 2359300
  179.5 1.4 copy-start.2
  180.9 1.4 copy-start.1
  182.3 1.4 copy-start

commit v2 on v1

--- a/solution.py
+++ b/solution.py
@@ -31,7 +31,8 @@
 def kernel(
     tiles, inner, outer, per_dev, cap,
     tok, gain, route_t, gates_t, w_gate, w_up, w_down, dmix,
-    mixed, grad_gates, grad_tok, out_gate, out_up, out_dn,
+    mixed_h, grad_gates_h, grad_tok_h, out_gate_h, out_up_h, out_dn_h,
+    mixed, grad_gates, grad_tok, out_gate, out_up, out_dn, out_sem,
     wgu, wdn, xs, xr, yr, ggu, gdn, rgu, rdn, fgu, fdn, tgu, tdn, prep, tmp, acc, cols, slot_r,
     load_sem, sw_send, sw_recv, ag_send, ag_recv, rs_send, rs_recv, fs_send, fs_recv,
     go_send, go_recv, go_own, back_send, back_recv, back_own,
@@ -268,9 +269,6 @@
         for events in lists:
             for place, event in events:
                 pl.when(i == place)(event)
-
-    def spread(count, makers):
-        return [(min(i, count - 1), maker) for i, maker in enumerate(makers)]
 
     for e in range(per_dev):
         for part in order:
@@ -330,85 +328,91 @@
         spread_of = jnp.mean(centred * centred, axis=-1, keepdims=True)
         prep[span, 0:feats] = (x * lax.rsqrt(spread_of + 1e-05) * gain[...]).astype(BF16)
         prep[span, feats : 2 * feats] = dmix[span, :]
-        service(i, [
-            (min(1, blocks - 1), lambda: ag_own(0, 0)),
-            (blocks - 1, lambda: ag_own(2, 0)),
-        ])
+        service(i, [(max(0, blocks - 2), lambda: ag_own(0, 0))])
         return carry
 
-    lax.fori_loop(0, blocks, slots, 0)
-    packs = per_dev * tiles
-
-    def pack(i, carry):
-        e, jt = i // tiles, lax.rem(i, tiles)
-        dest = lax.rem(t + jt, tiles)
-        want = lax.broadcasted_iota(jnp.int32, (wide, rows), 0) + (e * group + dest * inner) * cap
-        first = slot_r[0:1, :] == want
-        second = slot_r[1:2, :] == want
-        weight = jnp.where(first, gates_t[0:1, :], jnp.where(second, gates_t[1:2, :], 0.0))
-        scale = jnp.sum(weight, axis=1, keepdims=True)
-        got = matmul(onehot(jnp.logical_or(first, second)), prep[...])
-        xs[e, jt, :, :, 0:feats] = got[:, 0:feats].astype(BF16).reshape(inner, cap, feats)
-        xs[e, jt, :, :, feats : 2 * feats] = (
-            (scale * got[:, feats : 2 * feats]).astype(BF16).reshape(inner, cap, feats)
-        )
-        exchange(e, jt, begin, False, False)
-
-        @pl.when(both(jt == tiles - 1, e + 1 < per_dev))
-        def _():
-            swap_start(e + 1)
-
-        events = []
-        for s in range(outer - 1):
-            events.append((min(2 * s + 1, packs - 1), functools.partial(ag_event, 0, 0, s)))
-            if s == min(1, outer - 2):
-                events.append((min(2 * s + 1, packs - 1), lambda: ag_own(1, 0)))
-            events.append((min(2 * s + 2, packs - 1), functools.partial(ag_event, 2, 0, s)))
-        service(i, events)
-        return carry
-
-    lax.fori_loop(0, packs, pack, 0)
-
-    def later(condition, event):
-        return lambda: pl.when(condition)(event)
+    class Steps:
+        def __init__(self, events):
+            self.events = list(events)
+
+        def run(self, count=1):
+            for event in self.events[:count]:
+                event()
+            self.events = self.events[count:]
+
+        def rest(self):
+            self.run(len(self.events))
+
+        def pop(self):
+            event = self.events[0]
+            self.events = self.events[1:]
+            return event
+
+    gathers = {
+        (part, e): Steps(functools.partial(ag_event, part, e, s) for s in range(outer - 1))
+        for part in range(3) for e in range(per_dev)
+    }
+    reductions = {
+        (part, e): Steps(functools.partial(rs_event, part, e, step) for step in range(1, outer - 1))
+        for part in range(3) for e in range(per_dev)
+    }
+
+    def pack(e, queue):
+        def one(jt, carry):
+            dest = lax.rem(t + jt, tiles)
+            want = lax.broadcasted_iota(jnp.int32, (wide, rows), 0) + (e * group + dest * inner) * cap
+            first = slot_r[0:1, :] == want
+            second = slot_r[1:2, :] == want
+            weight = jnp.where(first, gates_t[0:1, :], jnp.where(second, gates_t[1:2, :], 0.0))
+            scale = jnp.sum(weight, axis=1, keepdims=True)
+            got = matmul(onehot(jnp.logical_or(first, second)), prep[...])
+            xs[e, jt, :, :, 0:feats] = got[:, 0:feats].astype(BF16).reshape(inner, cap, feats)
+            xs[e, jt, :, :, feats : 2 * feats] = (
+                (scale * got[:, feats : 2 * feats]).astype(BF16).reshape(inner, cap, feats)
+            )
+            if e == 0:
+                exchange(e, jt, begin, False, False)
+            service(jt, [(place, event) for place, event in enumerate(queue[:tiles]) if event])
+            return carry
+
+        lax.fori_loop(0, tiles, one, 0)
+        for event in queue[tiles:]:
+            event()
 
     def inputs(e, i):
         return xr[e, i, :, :, 0:feats].reshape(wide, feats), xr[e, i, :, :, feats : 2 * feats].reshape(wide, feats)
 
-    def expert(e, carry):
-        more = e + 1 < per_dev
-        before = e >= 1
-
-        def forward(h, events):
-            span_h = slice(h * half, (h + 1) * half)
-            deeper = blks // 2
-
-            def one(i, carry):
-                span = pl.ds(pl.multiple_of(i * wide, wide), wide)
-                x, d = inputs(e, i)
-                gate_pre = matmul(x, wgu[e, h, 0].reshape(feats, half))
-                up_pre = matmul(x, wgu[e, h, 1].reshape(feats, half))
-                down = wdn[e, h * deeper : (h + 1) * deeper].reshape(half, feats)
-                d_act = matmul(d, down, ((1,), (1,)))
-                sigma = jax.nn.sigmoid(gate_pre)
-                swish = gate_pre * sigma
-                tmp[0, span, span_h] = (swish * up_pre).astype(BF16)
-                tmp[1, span, span_h] = (d_act * up_pre * sigma * (1.0 + gate_pre * (1.0 - sigma))).astype(BF16)
-                tmp[2, span, span_h] = (d_act * swish).astype(BF16)
-                service(i, *events)
-                return carry
-
-            lax.fori_loop(0, tiles, one, 0)
-
-        def grads(h):
-            x_all = xr[e, :, :, :, 0:feats].reshape(many, feats)
-            for g in range(2):
-                grad = matmul(x_all, tmp[1 + g, :, h * half : (h + 1) * half], ((0,), (0,)))
-                ggu[e, h, g] = grad.astype(BF16).reshape(blks, thin, half)
-
-        width = min(256, hid)
-
-        def downs(i, carry):
+    def forward(e, h):
+        span_h = slice(h * half, (h + 1) * half)
+        deeper = blks // 2
+
+        def one(i, carry):
+            span = pl.ds(pl.multiple_of(i * wide, wide), wide)
+            x, d = inputs(e, i)
+            gate_pre = matmul(x, wgu[e, h, 0].reshape(feats, half))
+            up_pre = matmul(x, wgu[e, h, 1].reshape(feats, half))
+            down = wdn[e, h * deeper : (h + 1) * deeper].reshape(half, feats)
+            d_act = matmul(d, down, ((1,), (1,)))
+            sigma = jax.nn.sigmoid(gate_pre)
+            swish = gate_pre * sigma
+            tmp[0, span, span_h] = (swish * up_pre).astype(BF16)
+            tmp[1, span, span_h] = (d_act * up_pre * sigma * (1.0 + gate_pre * (1.0 - sigma))).astype(BF16)
+            tmp[2, span, span_h] = (d_act * swish).astype(BF16)
+            return carry
+
+        lax.fori_loop(0, tiles, one, 0)
+
+    def grads(e, h):
+        x_all = xr[e, :, :, :, 0:feats].reshape(many, feats)
+        for g in range(2):
+            grad = matmul(x_all, tmp[1 + g, :, h * half : (h + 1) * half], ((0,), (0,)))
+            ggu[e, h, g] = grad.astype(BF16).reshape(blks, thin, half)
+        rs_start(h, e)
+
+    width = min(256, hid)
+
+    def downs(e):
+        def one(i, carry):
             span = pl.ds(pl.multiple_of(i * width, width), width)
             d_all = xr[e, :, :, :, feats : 2 * feats].reshape(many, feats)
             grad = matmul(tmp[0, :, span], d_all, ((0,), (0,)))
@@ -416,7 +420,11 @@
             gdn[e, pl.ds(i * count, count)] = grad.astype(BF16).reshape(count, deep, feats)
             return carry
 
-        def back(ii, carry):
+        lax.fori_loop(0, hid // width, one, 0)
+        rs_start(2, e)
+
+    def back(e):
+        def one(ii, carry):
             jt = lax.rem(ii + 1, tiles)
             i = lax.rem(t + jt, tiles)
             span = pl.ds(pl.multiple_of(i * wide, wide), wide)
@@ -431,59 +439,74 @@
             xr[e, i, :, :, 0:feats] = out.astype(BF16).reshape(inner, cap, feats)
             xr[e, i, :, :, feats : 2 * feats] = d_in.astype(BF16).reshape(inner, cap, feats)
             exchange(e, jt, begin, True, False)
-            service(ii, *back_events)
             return carry
 
-        def ags(part, e, condition=None):
-            events = [functools.partial(ag_event, part, e, s) for s in range(outer - 1)]
-            if condition is not None:
-                events = [later(condition, event) for event in events]
-            return spread(tiles, events)
-
+        lax.fori_loop(0, tiles, one, 0)
+
+    lax.fori_loop(0, blocks, slots, 0)
+    ag_own(2, 0)
+    keys = sorted((s + (0.0, 1.2, 0.6)[part], part) for s in range(outer - 1) for part in range(3))
+    queue = [None]
+    for key, part in keys[:-2]:
+        queue.append(gathers[part, 0].pop())
+        if len(queue) == 2:
+            queue.append(lambda: ag_own(1, 0))
+    pack(0, queue[:tiles] if per_dev > 1 else queue)
+    for e in range(1, per_dev):
+        swap_start(e)
+        pack(e, queue[tiles:] if e == 1 else [])
+
+    for e in range(per_dev):
+        more, before = e + 1 < per_dev, e > 0
+        gathers[0, e].rest()
+        if more:
+            ag_own(0, e + 1)
+        gathers[2, e].rest()
+        if more:
+            ag_own(2, e + 1)
+            gathers[1, e].run()
+            ag_own(1, e + 1)
         everywhere(e, arrive, False, True)
-
-        @pl.when(more)
-        def _():
-            ag_own(0, e + 1)
-
-        tails = [later(before, event) for event in tail_events(e - 1)]
-        forward(0, [ags(1, e), spread(tiles, tails)])
-        grads(0)
-        rs_start(0, e)
-
-        @pl.when(more)
-        def _():
-            ag_own(2, e + 1)
-
-        steps = [functools.partial(rs_event, 0, e, step) for step in range(1, outer - 1)]
-        forward(1, [
-            ags(0, e + 1, more),
-            [(min(2 * i + 1, tiles - 1), event) for i, event in enumerate(steps)],
-        ])
-        grads(1)
-        rs_start(1, e)
-        lax.fori_loop(0, hid // width, downs, 0)
-        rs_start(2, e)
-        rs_final(0, e)
-
-        @pl.when(more)
-        def _():
-            ag_own(1, e + 1)
-
-        steps = []
-        for step in range(1, outer - 1):
-            steps += [functools.partial(rs_event, 1, e, step), functools.partial(rs_event, 2, e, step)]
-        back_events = [ags(2, e + 1, more), spread(tiles, steps), [(tiles - 1, lambda: rs_take(0, e))]]
-        lax.fori_loop(0, tiles, back, 0)
-        return carry
-
-    def tail_events(e):
-        return [
-            functools.partial(rs_final, 1, e), functools.partial(rs_final, 2, e),
-            functools.partial(rs_take, 1, e), functools.partial(rs_take, 2, e),
-        ]
-
-    lax.fori_loop(0, per_dev, expert, 0)
+        if more:
+            everywhere(e + 1, begin, False, False)
+        forward(e, 0)
+        if not before:
+            gathers[1, e].rest()
+        if more:
+            gathers[0, e + 1].run()
+        if before:
+            rs_final(1, e - 1)
+        grads(e, 0)
+        if before:
+            reductions[2, e - 1].run()
+            gathers[1, e].run()
+            reductions[2, e - 1].rest()
+            gathers[1, e].rest()
+        if more:
+            gathers[2, e + 1].run()
+            gathers[0, e + 1].run()
+        forward(e, 1)
+        if more:
+            gathers[1, e + 1].run()
+            gathers[2, e + 1].run()
+            gathers[0, e + 1].rest()
+        if before:
+            rs_final(2, e - 1)
+            rs_take(1, e - 1)
+        grads(e, 1)
+        reductions[0, e].run()
+        downs(e)
+        if more:
+            gathers[1, e + 1].run()
+        back(e)
+        if more:
+            reductions[0, e].rest()
+            gathers[2, e + 1].rest()
+            rs_final(0, e)
+            reductions[1, e].rest()
+            rs_take(0, e)
+            if before:
+                rs_take(2, e - 1)
 
     few = min(256, rows)
 
@@ -499,26 +522,41 @@
         dn = matmul(first + second, value[:, feats : 2 * feats])
         return span, column, y0, y1, dn
 
-    def early(e, carry):
-        everywhere(e, arrive, True, True)
-
+    def early(e):
         def one(i, carry):
             span, column, y0, y1, dn = gather(i, e)
             for k, value in enumerate((y0, y1, dn)):
                 lanes = slice(k * feats, (k + 1) * feats)
-                old = jnp.where(e == 0, 0.0, acc[span, lanes])
-                acc[span, lanes] = old + value
+                acc[span, lanes] = value + acc[span, lanes] if e else value
             return carry
 
+        everywhere(e, arrive, True, True)
         lax.fori_loop(0, rows // few, one, 0)
-        return carry
-
-    lax.fori_loop(0, per_dev - 1, early, 0)
+
     last = per_dev - 1
-    ending = tail_events(last)
-    ending[0]()
-    ending[1]()
+    reductions[0, last].rest()
+    rs_final(0, last)
+    for e in range(last):
+        early(e)
+    if last:
+        rs_take(2, last - 1)
+    reductions[1, last].rest()
+    rs_final(1, last)
+    reductions[2, last].run()
     everywhere(last, arrive, True, True)
+
+    results = [
+        pltpu.make_async_copy(src, dst, out_sem.at[i])
+        for i, (src, dst) in enumerate((
+            (mixed, mixed_h), (grad_gates, grad_gates_h), (grad_tok, grad_tok_h),
+            (out_gate, out_gate_h), (out_up, out_up_h), (out_dn, out_dn_h),
+        ))
+    ]
+    for part in range(2):
+        rs_take(part, last)
+    for copy in results[3:5]:
+        copy.start()
+    ending = [reductions[2, last].rest, functools.partial(rs_final, 2, last)]
 
     def finish(i, carry):
         span, column, y0, y1, dn = gather(i, last)
@@ -539,11 +577,14 @@
         u = dn * gain[...]
         pull = jnp.sum(u * x, axis=-1, keepdims=True) * (scale * scale * scale) / feats
         grad_tok[span, :] = (u * scale - pull * centred).astype(BF16)
+        service(i, [(min(2 * place, rows // few - 1), event) for place, event in enumerate(ending)])
         return carry
 
     lax.fori_loop(0, rows // few, finish, 0)
-    ending[2]()
-    ending[3]()
+    for copy in results[:3]:
+        copy.start()
+    rs_take(2, last)
+    results[5].start()
 
     def drain(e, carry):
         everywhere(e, leave, False, False)
@@ -567,6 +608,23 @@
         return carry
 
     lax.fori_loop(0, per_dev, drain, 0)
+    for copy in results:
+        copy.wait()
+
+
+def hand_over(*refs):
+    count = len(refs) // 3
+    stage, sems = refs[2 * count : 3 * count], refs[3 * count]
+    count_of = range(count)
+    into = [pltpu.make_async_copy(refs[i], stage[i], sems.at[0, i]) for i in count_of]
+    out = [pltpu.make_async_copy(stage[i], refs[count + i], sems.at[1, i]) for i in count_of]
+    for copy in into:
+        copy.start()
+    for first, second in zip(into, out):
+        first.wait()
+        second.start()
+    for copy in out:
+        copy.wait()
 
 
 def on_device(tiles, blks, tokens, ln_gain, route, gates, w_gate, w_up, w_down, d_mixed):
@@ -582,6 +640,7 @@
     many = tiles * inner * cap
     vmem = pl.BlockSpec(memory_space=pltpu.VMEM)
     hbm = pl.BlockSpec(memory_space=pl.ANY)
+    fixed = pl.BlockSpec(memory_space=pltpu.HBM)
     dma = pltpu.SemaphoreType.DMA
     outs = pl.pallas_call(
         functools.partial(kernel, tiles, inner, outer, per_dev, cap),
@@ -594,8 +653,15 @@
             jax.ShapeDtypeStruct((per_tile, deep, feats), F32),
         ),
         in_specs=[vmem, vmem, vmem, vmem, hbm, hbm, hbm, vmem],
-        out_specs=[vmem] * 6,
+        out_specs=[fixed] * 6,
         scratch_shapes=[
+            pltpu.VMEM((rows, feats), BF16),
+            pltpu.VMEM((2, rows), F32),
+            pltpu.VMEM((rows, feats), BF16),
+            pltpu.VMEM((per_tile, thin, hid), F32),
+            pltpu.VMEM((per_tile, thin, hid), F32),
+            pltpu.VMEM((per_tile, deep, feats), F32),
+            dma((6,)),
             pltpu.VMEM((per_dev, 2, 2, blks, thin, half), BF16),
             pltpu.VMEM((per_dev, blks, deep, feats), BF16),
             pltpu.VMEM((per_dev, tiles, inner, cap, 2 * feats), BF16),
@@ -634,6 +700,14 @@
             collective_id=0, has_side_effects=True, vmem_limit_bytes=67043328
         ),
     )(tokens, ln_gain.reshape(1, feats), route.T, gates.T, w_gate, w_up, w_down, d_mixed)
+    outs = pl.pallas_call(
+        hand_over,
+        out_shape=tuple(jax.ShapeDtypeStruct(out.shape, out.dtype) for out in outs),
+        in_specs=[fixed] * 6,
+        out_specs=[fixed] * 6,
+        scratch_shapes=[pltpu.VMEM(out.shape, out.dtype) for out in outs] + [dma((2, 6))],
+        compiler_params=pltpu.CompilerParams(vmem_limit_bytes=67043328),
+    )(*outs)
     return (outs[0], outs[1].T) + tuple(outs[2:])
 
 

time: 185 us -> 176 us (0.951)
  local copies, waits for them, and re-layouts: 9.14 us -> 1.24 us
  Pallas kernels: 175 us -> 173 us
    unnamed x18 -> x2, local copies, waits for them, and re-layouts: 8.57 us -> 0.67 us
    pallas_call x1, Pallas kernels: 175 us -> 170 us  [on_device(): pl.pallas_call(functools.partial(kernel, tiles, inner, outer, per_dev, ca...]
    pallas_call x0 -> x1, Pallas kernels: none -> 3.2 us  [on_device(): pl.pallas_call(hand_over, out_shape=tuple((jax.ShapeDtypeStruct(out.shape...]
where the time goes in v2:
time: 176 us; the launch traced here: 175 us
  Pallas kernels  173 us (98%)
    pallas_call x1, Pallas kernels, on_device(): pl.pallas_call(functools.partial(kernel, tiles, inner, outer, per_dev, ca...  170 us

profile of v2, /device:TPU:0, one launch (start us, length us, event | category | flops | bytes accessed | tf_op | source)
XLA Modules:
  0.0 175.4 jit_solution(14878170766682361825)
XLA Ops:
  0.6 0.0 copy-start
  0.6 0.7 copy-done
  1.3 0.6 reshape.15.gain
  1.9 170.1 %shard_map.127 = (bf16[1024,384]{1,0:T(8,128)(2,1)}, f32[2,1024]{1,0:T(2,128)}, bf16[1024,384]{1,0:T(8,128)(2,1)}, f32[4,48,1024]{2,1,0:T(8,128)}, f32[4,48,1024]{2,1,0:T(8,128)}, /*index=5*/f32[4,128,384]{2,1,0:T(8,128)}) custom-call(bf16[1024,384]{1,0:T(8,128)(2,1)} %tok.1, f32[1,384]{1,0:T(1,128)} %reshape.15.gain, s32[2,1024]{1,0:T(2,128)} %bitcast.3, ...), custom_call_target="tpu_custom_call" | custom-call | tf_op jit(solution)/shard_map/pallas_call | solution.py:645
  172.0 3.2 %shard_map.128 = (bf16[1024,384]{1,0:T(8,128)(2,1)}, f32[2,1024]{1,0:T(2,128)}, bf16[1024,384]{1,0:T(8,128)(2,1)}, f32[4,48,1024]{2,1,0:T(8,128)}, f32[4,48,1024]{2,1,0:T(8,128)}, /*index=5*/f32[4,128,384]{2,1,0:T(8,128)}) custom-call(bf16[1024,384]{1,0:T(8,128)(2,1)} %get-tuple-element.18.refs_0_, f32[2,1024]{1,0:T(2,128)} %get-tuple-element.19.refs_1_, ...), custom_call_target="tpu_custom_call" | custom-call | tf_op jit(solution)/shard_map/pallas_call | solution.py:703
Async XLA Ops:
  0.6 0.7 copy-start

commit v3 on v2

--- a/solution.py
+++ b/solution.py
@@ -492,7 +492,6 @@
             gathers[0, e + 1].rest()
         if before:
             rs_final(2, e - 1)
-            rs_take(1, e - 1)
         grads(e, 1)
         reductions[0, e].run()
         downs(e)
@@ -504,9 +503,6 @@
             gathers[2, e + 1].rest()
             rs_final(0, e)
             reductions[1, e].rest()
-            rs_take(0, e)
-            if before:
-                rs_take(2, e - 1)
 
     few = min(256, rows)
 
@@ -538,8 +534,6 @@
     rs_final(0, last)
     for e in range(last):
         early(e)
-    if last:
-        rs_take(2, last - 1)
     reductions[1, last].rest()
     rs_final(1, last)
     reductions[2, last].run()
@@ -552,10 +546,9 @@
             (out_gate, out_gate_h), (out_up, out_up_h), (out_dn, out_dn_h),
         ))
     ]
-    for part in range(2):
-        rs_take(part, last)
-    for copy in results[3:5]:
-        copy.start()
+    for e in range(last):
+        for part in range(3):
+            rs_take(part, e)
     ending = [reductions[2, last].rest, functools.partial(rs_final, 2, last)]
 
     def finish(i, carry):
@@ -583,8 +576,10 @@
     lax.fori_loop(0, rows // few, finish, 0)
     for copy in results[:3]:
         copy.start()
-    rs_take(2, last)
-    results[5].start()
+    for part in range(3):
+        rs_take(part, last)
+    for copy in results[3:]:
+        copy.start()
 
     def drain(e, carry):
         everywhere(e, leave, False, False)

time: 176 us -> 163 us (0.926)
  Pallas kernels: 173 us -> 160 us
    pallas_call x1, Pallas kernels: 170 us -> 157 us  [on_device(): pl.pallas_call(functools.partial(kernel, tiles, inner, outer, per_dev, ca...]
where the time goes in v3:
time: 163 us; the launch traced here: 162 us
  Pallas kernels  160 us (98%)
    pallas_call x1, Pallas kernels, on_device(): pl.pallas_call(functools.partial(kernel, tiles, inner, outer, per_dev, ca...  157 us

profile of v3, /device:TPU:0, one launch (start us, length us, event | category | flops | bytes accessed | tf_op | source)
XLA Modules:
  0.0 162.4 jit_solution(5508974144765388742)
XLA Ops:
  0.6 0.0 copy-start
  0.6 0.7 copy-done
  1.3 0.6 reshape.15.gain
  1.9 157.1 %shard_map.127 = (bf16[1024,384]{1,0:T(8,128)(2,1)}, f32[2,1024]{1,0:T(2,128)}, bf16[1024,384]{1,0:T(8,128)(2,1)}, f32[4,48,1024]{2,1,0:T(8,128)}, f32[4,48,1024]{2,1,0:T(8,128)}, /*index=5*/f32[4,128,384]{2,1,0:T(8,128)}) custom-call(bf16[1024,384]{1,0:T(8,128)(2,1)} %tok.1, f32[1,384]{1,0:T(1,128)} %reshape.15.gain, s32[2,1024]{1,0:T(2,128)} %bitcast.3, ...), custom_call_target="tpu_custom_call" | custom-call | tf_op jit(solution)/shard_map/pallas_call | solution.py:640
  159.0 3.2 %shard_map.128 = (bf16[1024,384]{1,0:T(8,128)(2,1)}, f32[2,1024]{1,0:T(2,128)}, bf16[1024,384]{1,0:T(8,128)(2,1)}, f32[4,48,1024]{2,1,0:T(8,128)}, f32[4,48,1024]{2,1,0:T(8,128)}, /*index=5*/f32[4,128,384]{2,1,0:T(8,128)}) custom-call(bf16[1024,384]{1,0:T(8,128)(2,1)} %get-tuple-element.18.refs_0_, f32[2,1024]{1,0:T(2,128)} %get-tuple-element.19.refs_1_, ...), custom_call_target="tpu_custom_call" | custom-call | tf_op jit(solution)/shard_map/pallas_call | solution.py:698
Async XLA Ops:
  0.6 0.7 copy-start
